TPU v7x, 32 devices: a whole 2x2x4 slice. The times are simulated.
32 devices in a mesh: expert: 8 (over z, x), dp: 4 (over y, core).
Axes of the slice: x: 2, y: 2, z: 4, core: 2. Of those that a mesh axis runs over, the one named last changes fastest.
Arguments:
- tokens: bfloat16 [1024, 7168], P('expert'), may hold values from -6 to 6
- routes: int32 [1024, 2], P('expert'), may hold values from 0 to 7, all different within a row; in each aligned block of 128 rows (0 to 127, 128 to 255, ...) at most 96 rows name the same one
- route_gates: bfloat16 [1024, 2], P('expert'), may hold values from 0.049804688 to 1
- cotangent: bfloat16 [1024, 7168], P('expert'), may hold values from -6 to 6
- weight_gate: bfloat16 [8, 7168, 1024], P('expert', None, 'dp'), may hold values from -0.0625 to 0.0625
- weight_up: bfloat16 [8, 7168, 1024], P('expert', None, 'dp'), may hold values from -0.0625 to 0.0625
- weight_down: bfloat16 [8, 1024, 7168], P('expert', 'dp'), may hold values from -0.1875 to 0.1875
Outputs:
- grad_tokens: bfloat16 [1024, 7168], P('expert', 'dp')
- grad_gate: bfloat16 [8, 7168, 1024], P('expert', None, 'dp')
- grad_up: bfloat16 [8, 7168, 1024], P('expert', None, 'dp')
- grad_down: bfloat16 [8, 1024, 7168], P('expert', 'dp')
Inputs may be any that keep to these rules, and one draw needn't show every extreme that they name: `routes`: within each aligned block of 128 rows (the tokens of one index of the expert axis) every row names 2 different experts and no expert is named by more than 96 rows; in every draw some block names some expert exactly 96 times.
All inputs are finite; a program needn't handle non-finite values.
Results may differ from a plain program's by a relative error of at most 0.011.
Values may be sent and summed in bfloat16 or wider, within the bound.
A program may use at most 192 MiB of HBM per device.

v0:
```python
import jax
import jax.numpy as jnp
from jax import lax
from jax.sharding import PartitionSpec as P


def slot_layout(routes, experts, capacity):
    flat_routes = routes.reshape(-1)
    onehot = (flat_routes[:, None] == jnp.arange(experts, dtype=jnp.int32)[None, :]).astype(
        jnp.int32
    )
    before = jnp.cumsum(onehot, axis=0) - onehot
    position = jnp.sum(before * onehot, axis=1)
    slot_index = flat_routes * capacity + position
    total_slots = flat_routes.shape[0]
    owners = (
        jnp.full((experts * capacity,), total_slots, dtype=jnp.int32)
        .at[slot_index]
        .set(jnp.arange(total_slots, dtype=jnp.int32))
    )
    return (slot_index, owners)


def pad_rows(source_array, owners, top_count):
    extended = jnp.concatenate(
        [source_array, jnp.zeros((1,) + source_array.shape[1:], source_array.dtype)], 0
    )
    return extended[owners // top_count]


def per_device(tokens, routes, route_gates, cotangent, weight_gate, weight_up, weight_down):
    members = lax.axis_size("expert")
    groups = lax.axis_size("dp")
    local_experts = weight_gate.shape[0]
    experts = members * local_experts
    token_rows = routes.shape[0]
    top_count = routes.shape[1]
    width = tokens.shape[1]
    quarter = width // groups
    capacity = 3 * token_rows * top_count // experts
    slot_index, owners = slot_layout(routes, experts, capacity)
    gate_flat = jnp.concatenate([route_gates.reshape(-1), jnp.zeros((1,), route_gates.dtype)], 0)
    gate_send = gate_flat[owners].reshape(experts, capacity)
    token_send = pad_rows(tokens, owners, top_count).reshape(experts, capacity, width)
    back_send = pad_rows(cotangent, owners, top_count).reshape(experts, capacity, width)
    token_arrived, back_arrived, gate_arrived = (
        lax.all_to_all(token_send, "expert", split_axis=0, concat_axis=1, tiled=True),
        lax.all_to_all(back_send, "expert", split_axis=0, concat_axis=1, tiled=True),
        lax.all_to_all(gate_send, "expert", split_axis=0, concat_axis=1, tiled=True),
    )
    scale = gate_arrived.astype(jnp.float32)[:, :, None]
    pre_gate = jnp.einsum(
        "erd,edf->erf", token_arrived, weight_gate, preferred_element_type=jnp.float32
    )
    pre_up = jnp.einsum(
        "erd,edf->erf", token_arrived, weight_up, preferred_element_type=jnp.float32
    )
    sigma = jax.nn.sigmoid(pre_gate)
    activated = pre_gate * sigma
    scaled_hidden = (scale * activated * pre_up).astype(jnp.bfloat16)
    back_hidden = scale * jnp.einsum(
        "erd,efd->erf", back_arrived, weight_down, preferred_element_type=jnp.float32
    )
    back_up = (back_hidden * activated).astype(jnp.bfloat16)
    back_gate = (back_hidden * pre_up * sigma * (1.0 + pre_gate * (1.0 - sigma))).astype(
        jnp.bfloat16
    )
    grad_gate = jnp.einsum(
        "erd,erf->edf", token_arrived, back_gate, preferred_element_type=jnp.float32
    ).astype(jnp.bfloat16)
    grad_up = jnp.einsum(
        "erd,erf->edf", token_arrived, back_up, preferred_element_type=jnp.float32
    ).astype(jnp.bfloat16)
    grad_down = jnp.einsum(
        "erf,erd->efd", scaled_hidden, back_arrived, preferred_element_type=jnp.float32
    ).astype(jnp.bfloat16)
    up_term = jnp.einsum("edf,erf->der", weight_up, back_up, preferred_element_type=jnp.float32)
    gate_term = jnp.einsum(
        "edf,erf->der", weight_gate, back_gate, preferred_element_type=jnp.float32
    )
    slot_back = lax.psum_scatter(
        (up_term + gate_term).astype(jnp.bfloat16), "dp", scatter_dimension=0, tiled=True
    )
    returned = lax.all_to_all(slot_back, "expert", split_axis=2, concat_axis=1, tiled=True)
    flat_back = returned.reshape(quarter, experts * capacity)
    picked = (
        jnp.take(flat_back, slot_index, axis=1)
        .astype(jnp.float32)
        .reshape(quarter, token_rows, top_count)
    )
    grad_tokens = jnp.sum(picked, axis=2).T.astype(jnp.bfloat16)
    return (grad_tokens, grad_gate, grad_up, grad_down)


def solution(mesh):
    placed = (
        P("expert", None),
        P("expert", None),
        P("expert", None),
        P("expert", None),
        P("expert", None, "dp"),
        P("expert", None, "dp"),
        P("expert", "dp", None),
    )
    return jax.shard_map(
        per_device,
        mesh=mesh,
        in_specs=placed,
        out_specs=(
            P("expert", "dp"),
            P("expert", None, "dp"),
            P("expert", None, "dp"),
            P("expert", "dp", None),
        ),
        check_vma=False,
    )
```

profile of v0, /device:TPU:0, one launch (start us, length us, event | category | flops | bytes accessed | tf_op | source)
XLA Modules:
  0.0 770.3 jit_solution(8576594936999472891)
XLA Ops:
  12.5 5.0 gather_fusion
  18.2 7.3 all-to-all-start
  27.2 9.4 %gather_fusion.2 = bf16[768,7168]{1,0:T(8,128)(2,1)} fusion(bf16[129,7168]{1,0:T(8,128)(2,1)S(1)} %concatenate.11, s32[1024]{0:T(1024)S(1)} %get-tuple-element.9), kind=kCustom, calls=%fused_computation.2 | custom fusion | bytes 22023168 | tf_op jit(solution)/shard_map/gather | solution.py:28
  36.6 6.0 all-to-all-start.2
  44.3 9.5 %gather_fusion.1 = bf16[768,7168]{1,0:T(8,128)(2,1)} fusion(bf16[129,7168]{1,0:T(8,128)(2,1)S(1)} %concatenate.10, s32[1024]{0:T(1024)S(1)} %get-tuple-element.9), kind=kCustom, calls=%fused_computation.1 | custom fusion | bytes 22023168 | tf_op jit(solution)/shard_map/gather | solution.py:28
  53.7 227.6 %all-to-all-done.2 = bf16[8,96,7168]{2,1,0:T(8,128)(2,1)} async-done(((bf16[8,96,7168]{2,1,0:T(8,128)(2,1)}), bf16[8,96,7168]{2,1,0:T(8,128)(2,1)}, u32[]{:S(2)}, u32[]{:S(2)}) %all-to-all-start.2) | async-done | bytes 11010080 | tf_op jit(solution)/shard_map/all_to_all | solution.py:47
  281.4 5.2 all-to-all-start.1
  287.0 6.9 fusion.4
  293.9 230.6 %all-to-all-done.1 = bf16[8,96,7168]{2,1,0:T(8,128)(2,1)} async-done(((bf16[8,96,7168]{2,1,0:T(8,128)(2,1)}), bf16[8,96,7168]{2,1,0:T(8,128)(2,1)}, u32[]{:S(2)}, u32[]{:S(2)}) %all-to-all-start.1) | async-done | bytes 11010080 | tf_op jit(solution)/shard_map/all_to_all | solution.py:48
  524.5 7.1 fusion.13
  531.6 8.3 %multiply_convert_fusion.1 = (bf16[768,256]{1,0:T(8,128)(2,1)S(1)}, bf16[768,256]{1,0:T(8,128)(2,1)S(1)}, f32[768,256]{1,0:T(8,128)}) fusion(f32[768,256]{1,0:T(8,128)S(1)} %fusion.13, f32[768,256]{1,0:T(8,128)S(1)} %fusion.4, bf16[768,7168]{1,0:T(8,128)(2,1)} %bitcast.8, bf16[1,7168,256]{2,1,0:T(8,128)(2,1)S(1)} %copy-done.1), kind=kOutput, calls=%fused_computation.27 | convolution fusion | flops 2821128192 | bytes 17825792 | tf_op jit(solution)/shard_map/erd,edf->erf/dot_general | solution.py:52
  540.0 9.1 %fusion.6 = f32[768,7168]{1,0:T(8,128)} fusion(bf16[768,256]{1,0:T(8,128)(2,1)S(1)} %get-tuple-element.5, bf16[1,7168,256]{2,1,0:T(8,128)(2,1)S(1)} %copy-done), kind=kOutput, calls=%fused_computation.15 | convolution fusion | flops 2818572288 | bytes 26083328 | tf_op jit(solution)/shard_map/edf,erf->der/dot_general | solution.py:77
  549.0 12.8 %fusion = bf16[7168,1,768]{0,2,1:T(8,128)(2,1)} fusion(f32[768,7168]{1,0:T(8,128)} %fusion.6, bf16[768,256]{1,0:T(8,128)(2,1)S(1)} %get-tuple-element.4, bf16[1,7168,256]{2,1,0:T(8,128)(2,1)S(1)} %copy-done.1), kind=kOutput, calls=%fused_computation.6 | convolution fusion | flops 2829582336 | bytes 37093376 | tf_op jit(solution)/shard_map/edf,erf->der/dot_general | solution.py:78
  561.9 88.4 %reduce-scatter.2.cloned.1.call-done = bf16[1792,1,768]{0,2,1:T(8,128)(2,1)} async-done(((bf16[7168,1,768]{0,2,1:T(8,128)(2,1)}), bf16[1792,1,768]{0,2,1:T(8,128)(2,1)}) %reduce-scatter.2.cloned.1.call-update) | async-done | bytes 2752528 | tf_op jit(solution)/shard_map/reduce_scatter | solution.py:81
  650.3 8.4 %copy.44 = bf16[1792,1,768]{0,1,2:T(2,128)(2,1)} copy(bf16[1792,1,768]{0,2,1:T(8,128)(2,1)} %reduce-scatter.2.cloned.1.call-done) | data formatting | bytes 5505024 | tf_op jit(solution)/shard_map/reduce_scatter | solution.py:81
  659.2 17.0 %reduce.7 = bf16[768,1792]{1,0:T(8,128)(2,1)S(1)} reduce(bf16[768,1,1792]{2,1,0:T(2,128)(2,1)} %bitcast.67, bf16[]{:T(256)} %broadcast.118), dimensions={1}, to_apply=%bitcast.62.reduce_sub_computation | reduce | bytes 5505026
  676.3 3.5 reshape.245
  679.7 5.7 all-to-all-start.3
  689.0 9.5 %fusion.3 = bf16[1,256,7168]{2,1,0:T(8,128)(2,1)} fusion(bf16[768,7168]{1,0:T(8,128)(2,1)} %bitcast.5, f32[768,256]{1,0:T(8,128)S(1)} %fusion.4, f32[768]{0:T(1024)S(1)} %reshape.191, f32[768,256]{1,0:T(8,128)} %get-tuple-element.8), kind=kOutput, calls=%fused_computation.12 | convolution fusion | flops 2821783552 | bytes 16256000 | tf_op jit(solution)/shard_map/erf,erd->efd/dot_general | solution.py:74
  698.5 9.1 %fusion.1 = bf16[1,7168,256]{2,1,0:T(8,128)(2,1)} fusion(bf16[768,7168]{1,0:T(8,128)(2,1)} %bitcast.8, bf16[768,256]{1,0:T(8,128)(2,1)S(1)} %copy-done.3), kind=kOutput, calls=%fused_computation.10 | convolution fusion | flops 2820407296 | bytes 15073280 | tf_op jit(solution)/shard_map/erd,erf->edf/dot_general | solution.py:68
  707.6 9.1 %fusion.2 = bf16[1,7168,256]{2,1,0:T(8,128)(2,1)} fusion(bf16[768,7168]{1,0:T(8,128)(2,1)} %bitcast.8, bf16[768,256]{1,0:T(8,128)(2,1)S(1)} %copy-done.5), kind=kOutput, calls=%fused_computation.11 | convolution fusion | flops 2820407296 | bytes 15073280 | tf_op jit(solution)/shard_map/erd,erf->edf/dot_general | solution.py:71
  716.7 31.0 %all-to-all-done.3 = bf16[8,2,86016]{2,1,0:T(2,128)(2,1)S(1)} async-done(((bf16[8,2,86016]{2,1,0:T(2,128)(2,1)}), bf16[8,2,86016]{2,1,0:T(2,128)(2,1)S(1)}, u32[]{:S(2)}, u32[]{:S(2)}) %all-to-all-start.3) | async-done | bytes 2752544 | tf_op jit(solution)/shard_map/all_to_all | solution.py:84
  747.7 4.9 reshape.246
  752.6 3.0 copy.43
  (53 shorter events, 21.5 us)
Async XLA Ops:
  18.2 18.3 %all-to-all-start = ((bf16[8,1,96]{2,1,0:T(2,128)(2,1)}), bf16[8,1,96]{2,1,0:T(2,128)(2,1)S(1)}, u32[]{:S(2)}, u32[]{:S(2)}) async-start(bf16[8,1,96]{2,1,0:T(2,128)(2,1)} %all_to_all.16), calls=%async_computation | async-start | bytes 8192 | tf_op jit(solution)/shard_map/all_to_all | solution.py:49
  36.6 244.8 %all-to-all-start.2 = ((bf16[8,96,7168]{2,1,0:T(8,128)(2,1)}), bf16[8,96,7168]{2,1,0:T(8,128)(2,1)}, u32[]{:S(2)}, u32[]{:S(2)}) async-start(bf16[8,96,7168]{2,1,0:T(8,128)(2,1)} %bitcast.65), calls=%async_computation.2 | async-start | bytes 22020096 | tf_op jit(solution)/shard_map/all_to_all | solution.py:47
  281.4 243.2 %all-to-all-start.1 = ((bf16[8,96,7168]{2,1,0:T(8,128)(2,1)}), bf16[8,96,7168]{2,1,0:T(8,128)(2,1)}, u32[]{:S(2)}, u32[]{:S(2)}) async-start(bf16[8,96,7168]{2,1,0:T(8,128)(2,1)} %bitcast.64), calls=%async_computation.1 | async-start | bytes 22020096 | tf_op jit(solution)/shard_map/all_to_all | solution.py:48
  286.6 363.7 %reduce-scatter.2.cloned.1.call-start = ((), (), s32[]{:S(2)}) async-start(), calls=%async_computation.5 | async-start | bytes 13762560 | tf_op jit(solution)/shard_map/reduce_scatter | solution.py:81
  524.5 7.1 copy-start.1
  531.6 8.3 %copy-start = (bf16[1,7168,256]{2,1,0:T(8,128)(2,1)S(1)}, bf16[1,7168,256]{2,1,0:T(8,128)(2,1)}, u32[]{:S(2)}) copy-start(bf16[1,7168,256]{2,1,0:T(8,128)(2,1)} %param.12) | copy-start | bytes 11010052
  540.0 9.1 %copy-start.4 = (bf16[768,256]{1,0:T(8,128)(2,1)}, bf16[768,256]{1,0:T(8,128)(2,1)S(1)}, u32[]{:S(2)}) copy-start(bf16[768,256]{1,0:T(8,128)(2,1)S(1)} %get-tuple-element.5) | copy-start | bytes 1179652
  540.0 9.1 %copy-start.2 = (bf16[768,256]{1,0:T(8,128)(2,1)}, bf16[768,256]{1,0:T(8,128)(2,1)S(1)}, u32[]{:S(2)}) copy-start(bf16[768,256]{1,0:T(8,128)(2,1)S(1)} %get-tuple-element.4) | copy-start | bytes 1179652
  676.2 10.9 %copy-start.7 = (s32[128,2]{0,1:T(2,128)S(1)}, s32[128,2]{0,1:T(2,128)}, u32[]{:S(2)}) copy-start(s32[128,2]{0,1:T(2,128)} %param.8) | copy-start | bytes 3076
  679.7 68.0 %all-to-all-start.3 = ((bf16[8,2,86016]{2,1,0:T(2,128)(2,1)}), bf16[8,2,86016]{2,1,0:T(2,128)(2,1)S(1)}, u32[]{:S(2)}, u32[]{:S(2)}) async-start(bf16[8,2,86016]{2,1,0:T(2,128)(2,1)} %reshape.245), calls=%async_computation.4 | async-start | bytes 5505024 | tf_op jit(solution)/shard_map/all_to_all | solution.py:84
  689.0 9.5 %copy-start.3 = (bf16[768,256]{1,0:T(8,128)(2,1)S(1)}, bf16[768,256]{1,0:T(8,128)(2,1)}, u32[]{:S(2)}) copy-start(bf16[768,256]{1,0:T(8,128)(2,1)} %copy-done.2) | copy-start | bytes 1179652
  698.5 9.1 %copy-start.5 = (bf16[768,256]{1,0:T(8,128)(2,1)S(1)}, bf16[768,256]{1,0:T(8,128)(2,1)}, u32[]{:S(2)}) copy-start(bf16[768,256]{1,0:T(8,128)(2,1)} %copy-done.4) | copy-start | bytes 1179652
  752.6 7.8 %copy-start.6 = (pred[128,2]{1,0:T(8,128)(4,1)S(1)}, pred[128,2]{1,0:T(8,128)(4,1)}, u32[]{:S(2)}) copy-start(pred[128,2]{1,0:T(8,128)(4,1)} %copy.33) | copy-start | bytes 772
Sparse Core Ops, SparseCore 0:
  562.0 88.2 reduce-scatter.1
where the time goes:
time: 776 us; the launch traced here: 770 us
  waiting for transfers between devices  578 us (74%)
  matrix products  71.9 us (9%)
  local copies, waits for them, and re-layouts  60 us (8%)
  starting transfers between devices  24.5 us (3%)
  other arithmetic  21.8 us (3%)
  between operations  14.5 us (2%)
    all_to_all x1, waiting for transfers between devices, per_device(): lax.all_to_all(back_send, 'expert', split_axis=0, concat_axis=1, tiled=True)  231 us
    all_to_all x1, waiting for transfers between devices, per_device(): lax.all_to_all(token_send, 'expert', split_axis=0, concat_axis=1, tiled=T...  228 us
    reduce_scatter x1, waiting for transfers between devices, per_device(): lax.psum_scatter((up_term + gate_term).astype(jnp.bfloat16), 'dp', scatte...  88.4 us
    all_to_all x1, waiting for transfers between devices, per_device(): lax.all_to_all(slot_back, 'expert', split_axis=2, concat_axis=1, tiled=True)  31 us
    gather x2, local copies, waits for them, and re-layouts, pad_rows(): return extended[owners // top_count]  18.9 us
    unnamed x1, other arithmetic  17 us
  transfers between devices with their start and end apart: 5, of which 4 were waited for; matrix products, arithmetic and copies ran while one was open for 8% of the time, Pallas kernels for 0%

commit v1 on v0

--- a/solution.py
+++ b/solution.py
@@ -1,7 +1,23 @@
+import functools
 import jax
 import jax.numpy as jnp
 from jax import lax
 from jax.sharding import PartitionSpec as P
+
+
+def show_the_slabs(buf, net_axis):
+    return jnp.concatenate(
+        lax.all_to_all(
+            jnp.stack(jnp.split(buf, lax.axis_size(net_axis), axis=2), axis=0),
+            split_axis=0,
+            concat_axis=0,
+            axis_name=net_axis,
+        ),
+        axis=1,
+    )
+
+
+set_windows = functools.partial(show_the_slabs, net_axis="expert")
 
 
 def slot_layout(routes, experts, capacity):
@@ -81,7 +97,7 @@
     slot_back = lax.psum_scatter(
         (up_term + gate_term).astype(jnp.bfloat16), "dp", scatter_dimension=0, tiled=True
     )
-    returned = lax.all_to_all(slot_back, "expert", split_axis=2, concat_axis=1, tiled=True)
+    returned = set_windows(slot_back)
     flat_back = returned.reshape(quarter, experts * capacity)
     picked = (
         jnp.take(flat_back, slot_index, axis=1)

time: 776 us -> 747 us (0.963)
  other arithmetic: 21.8 us -> 4.82 us
    unnamed x1 -> x0, other arithmetic: 17 us -> none
    reduce_scatter x1 -> x0, local copies, waits for them, and re-layouts: 8.41 us -> none  [per_device(): lax.psum_scatter((up_term + gate_term).astype(jnp.bfloat16), 'dp', scatte...]
where the time goes in v1:
time: 747 us; the launch traced here: 746 us
  waiting for transfers between devices  578 us (77%)
  matrix products  71.4 us (10%)
  local copies, waits for them, and re-layouts  53.4 us (7%)
  starting transfers between devices  24.2 us (3%)
  between operations  14.2 us (2%)
    all_to_all x1, waiting for transfers between devices, per_device(): lax.all_to_all(back_send, 'expert', split_axis=0, concat_axis=1, tiled=True)  231 us
    all_to_all x1, waiting for transfers between devices, per_device(): lax.all_to_all(token_send, 'expert', split_axis=0, concat_axis=1, tiled=T...  228 us
    reduce_scatter x1, waiting for transfers between devices, per_device(): lax.psum_scatter((up_term + gate_term).astype(jnp.bfloat16), 'dp', scatte...  88.4 us
    all_to_all x1, waiting for transfers between devices, show_the_slabs(): lax.all_to_all(jnp.stack(jnp.split(buf, lax.axis_size(net_axis), axis=2),...  31 us
    gather x2, local copies, waits for them, and re-layouts, pad_rows(): return extended[owners // top_count]  18.9 us
  transfers between devices with their start and end apart: 5, of which 4 were waited for; matrix products, arithmetic and copies ran while one was open for 8% of the time, Pallas kernels for 0%

profile of v1, /device:TPU:0, one launch (start us, length us, event | category | flops | bytes accessed | tf_op | source)
XLA Modules:
  0.0 745.9 jit_solution(13824162419636644597)
XLA Ops:
  12.5 5.0 gather_fusion
  18.2 7.3 all-to-all-start
  27.2 9.4 %gather_fusion.2 = bf16[768,7168]{1,0:T(8,128)(2,1)} fusion(bf16[129,7168]{1,0:T(8,128)(2,1)S(1)} %concatenate.11, s32[1024]{0:T(1024)S(1)} %get-tuple-element.9), kind=kCustom, calls=%fused_computation.2 | custom fusion | bytes 22023168 | tf_op jit(solution)/shard_map/gather | solution.py:44
  36.6 6.0 all-to-all-start.2
  44.3 9.5 %gather_fusion.1 = bf16[768,7168]{1,0:T(8,128)(2,1)} fusion(bf16[129,7168]{1,0:T(8,128)(2,1)S(1)} %concatenate.10, s32[1024]{0:T(1024)S(1)} %get-tuple-element.9), kind=kCustom, calls=%fused_computation.1 | custom fusion | bytes 22023168 | tf_op jit(solution)/shard_map/gather | solution.py:44
  53.7 227.6 %all-to-all-done.2 = bf16[8,96,7168]{2,1,0:T(8,128)(2,1)} async-done(((bf16[8,96,7168]{2,1,0:T(8,128)(2,1)}), bf16[8,96,7168]{2,1,0:T(8,128)(2,1)}, u32[]{:S(2)}, u32[]{:S(2)}) %all-to-all-start.2) | async-done | bytes 11010080 | tf_op jit(solution)/shard_map/all_to_all | solution.py:63
  281.4 5.2 all-to-all-start.1
  286.9 6.9 fusion.4
  293.8 230.7 %all-to-all-done.1 = bf16[8,96,7168]{2,1,0:T(8,128)(2,1)} async-done(((bf16[8,96,7168]{2,1,0:T(8,128)(2,1)}), bf16[8,96,7168]{2,1,0:T(8,128)(2,1)}, u32[]{:S(2)}, u32[]{:S(2)}) %all-to-all-start.1) | async-done | bytes 11010080 | tf_op jit(solution)/shard_map/all_to_all | solution.py:64
  524.5 7.1 fusion.13
  531.6 8.3 %multiply_convert_fusion.1 = (bf16[768,256]{1,0:T(8,128)(2,1)S(1)}, bf16[768,256]{1,0:T(8,128)(2,1)S(1)}, f32[768,256]{1,0:T(8,128)}) fusion(f32[768,256]{1,0:T(8,128)S(1)} %fusion.13, f32[768,256]{1,0:T(8,128)S(1)} %fusion.4, bf16[768,7168]{1,0:T(8,128)(2,1)} %bitcast.8, bf16[1,7168,256]{2,1,0:T(8,128)(2,1)S(1)} %copy-done.1), kind=kOutput, calls=%fused_computation.26 | convolution fusion | flops 2821128192 | bytes 17825792 | tf_op jit(solution)/shard_map/erd,edf->erf/dot_general | solution.py:68
  540.0 9.0 %fusion.6 = f32[768,7168]{1,0:T(8,128)} fusion(bf16[768,256]{1,0:T(8,128)(2,1)S(1)} %get-tuple-element.5, bf16[1,7168,256]{2,1,0:T(8,128)(2,1)S(1)} %copy-done), kind=kOutput, calls=%fused_computation.15 | convolution fusion | flops 2818572288 | bytes 26083328 | tf_op jit(solution)/shard_map/edf,erf->der/dot_general | solution.py:93
  549.0 12.3 %fusion = bf16[7168,1,768]{0,2,1:T(8,128)(2,1)} fusion(f32[768,7168]{1,0:T(8,128)} %fusion.6, bf16[768,256]{1,0:T(8,128)(2,1)S(1)} %get-tuple-element.4, bf16[1,7168,256]{2,1,0:T(8,128)(2,1)S(1)} %copy-done.1), kind=kOutput, calls=%fused_computation.6 | convolution fusion | flops 2829582336 | bytes 37093376 | tf_op jit(solution)/shard_map/edf,erf->der/dot_general | solution.py:94
  561.4 88.4 %reduce-scatter.2.cloned.1.call-done = bf16[1792,1,768]{0,2,1:T(8,128)(2,1)} async-done(((bf16[7168,1,768]{0,2,1:T(8,128)(2,1)}), bf16[1792,1,768]{0,2,1:T(8,128)(2,1)}) %reduce-scatter.2.cloned.1.call-update) | async-done | bytes 2752528 | tf_op jit(solution)/shard_map/reduce_scatter | solution.py:97
  651.5 1.8 fusion.25
  660.3 1.8 fusion.20
  663.7 5.5 all-to-all-start.3
  672.8 9.5 %fusion.3 = bf16[1,256,7168]{2,1,0:T(8,128)(2,1)} fusion(bf16[768,7168]{1,0:T(8,128)(2,1)} %bitcast.5, f32[768,256]{1,0:T(8,128)S(1)} %fusion.4, f32[768]{0:T(1024)S(1)} %reshape.187, f32[768,256]{1,0:T(8,128)} %get-tuple-element.8), kind=kOutput, calls=%fused_computation.12 | convolution fusion | flops 2821783552 | bytes 16256000 | tf_op jit(solution)/shard_map/erf,erd->efd/dot_general | solution.py:90
  682.3 9.1 %fusion.1 = bf16[1,7168,256]{2,1,0:T(8,128)(2,1)} fusion(bf16[768,7168]{1,0:T(8,128)(2,1)} %bitcast.8, bf16[768,256]{1,0:T(8,128)(2,1)S(1)} %copy-done.3), kind=kOutput, calls=%fused_computation.10 | convolution fusion | flops 2820407296 | bytes 15073280 | tf_op jit(solution)/shard_map/erd,erf->edf/dot_general | solution.py:84
  691.5 9.1 %fusion.2 = bf16[1,7168,256]{2,1,0:T(8,128)(2,1)} fusion(bf16[768,7168]{1,0:T(8,128)(2,1)} %bitcast.8, bf16[768,256]{1,0:T(8,128)(2,1)S(1)} %copy-done.5), kind=kOutput, calls=%fused_computation.11 | convolution fusion | flops 2820407296 | bytes 15073280 | tf_op jit(solution)/shard_map/erd,erf->edf/dot_general | solution.py:87
  700.5 31.0 %all-to-all-done.3 = bf16[8,1792,1,96]{1,3,2,0:T(8,128)(2,1)S(1)} async-done(((bf16[8,1792,1,96]{1,3,2,0:T(8,128)(2,1)}), bf16[8,1792,1,96]{1,3,2,0:T(8,128)(2,1)S(1)}, u32[]{:S(2)}, u32[]{:S(2)}) %all-to-all-start.3) | async-done | bytes 2752544 | tf_op jit(solution)/shard_map/all_to_all | solution.py:10
  731.6 2.3 gather_fusion.3
  733.8 2.3 gather.19
  736.2 2.8 fusion.16
  (55 shorter events, 23.7 us)
Async XLA Ops:
  18.2 18.3 %all-to-all-start = ((bf16[8,1,96]{2,1,0:T(2,128)(2,1)}), bf16[8,1,96]{2,1,0:T(2,128)(2,1)S(1)}, u32[]{:S(2)}, u32[]{:S(2)}) async-start(bf16[8,1,96]{2,1,0:T(2,128)(2,1)} %all_to_all.32), calls=%async_computation | async-start | bytes 8192 | tf_op jit(solution)/shard_map/all_to_all | solution.py:65
  36.6 244.8 %all-to-all-start.2 = ((bf16[8,96,7168]{2,1,0:T(8,128)(2,1)}), bf16[8,96,7168]{2,1,0:T(8,128)(2,1)}, u32[]{:S(2)}, u32[]{:S(2)}) async-start(bf16[8,96,7168]{2,1,0:T(8,128)(2,1)} %bitcast.92), calls=%async_computation.2 | async-start | bytes 22020096 | tf_op jit(solution)/shard_map/all_to_all | solution.py:63
  281.4 243.2 %all-to-all-start.1 = ((bf16[8,96,7168]{2,1,0:T(8,128)(2,1)}), bf16[8,96,7168]{2,1,0:T(8,128)(2,1)}, u32[]{:S(2)}, u32[]{:S(2)}) async-start(bf16[8,96,7168]{2,1,0:T(8,128)(2,1)} %bitcast.91), calls=%async_computation.1 | async-start | bytes 22020096 | tf_op jit(solution)/shard_map/all_to_all | solution.py:64
  286.6 363.2 %reduce-scatter.2.cloned.1.call-start = ((), (), s32[]{:S(2)}) async-start(), calls=%async_computation.5 | async-start | bytes 13762560 | tf_op jit(solution)/shard_map/reduce_scatter | solution.py:97
  524.5 7.1 copy-start.1
  531.6 8.3 %copy-start = (bf16[1,7168,256]{2,1,0:T(8,128)(2,1)S(1)}, bf16[1,7168,256]{2,1,0:T(8,128)(2,1)}, u32[]{:S(2)}) copy-start(bf16[1,7168,256]{2,1,0:T(8,128)(2,1)} %param.12) | copy-start | bytes 11010052
  540.0 9.1 %copy-start.4 = (bf16[768,256]{1,0:T(8,128)(2,1)}, bf16[768,256]{1,0:T(8,128)(2,1)S(1)}, u32[]{:S(2)}) copy-start(bf16[768,256]{1,0:T(8,128)(2,1)S(1)} %get-tuple-element.5) | copy-start | bytes 1179652
  540.0 9.1 %copy-start.2 = (bf16[768,256]{1,0:T(8,128)(2,1)}, bf16[768,256]{1,0:T(8,128)(2,1)S(1)}, u32[]{:S(2)}) copy-start(bf16[768,256]{1,0:T(8,128)(2,1)S(1)} %get-tuple-element.4) | copy-start | bytes 1179652
  660.2 10.7 %copy-start.7 = (s32[128,2]{0,1:T(2,128)S(1)}, s32[128,2]{0,1:T(2,128)}, u32[]{:S(2)}) copy-start(s32[128,2]{0,1:T(2,128)} %param.8) | copy-start | bytes 3076
  663.7 67.8 %all-to-all-start.3 = ((bf16[8,1792,1,96]{1,3,2,0:T(8,128)(2,1)}), bf16[8,1792,1,96]{1,3,2,0:T(8,128)(2,1)S(1)}, u32[]{:S(2)}, u32[]{:S(2)}) async-start(bf16[8,1792,1,96]{1,3,2,0:T(8,128)(2,1)} %fusion.19), calls=%async_computation.4 | async-start | bytes 5505024 | tf_op jit(solution)/shard_map/all_to_all | solution.py:10
  672.8 9.5 %copy-start.3 = (bf16[768,256]{1,0:T(8,128)(2,1)S(1)}, bf16[768,256]{1,0:T(8,128)(2,1)}, u32[]{:S(2)}) copy-start(bf16[768,256]{1,0:T(8,128)(2,1)} %copy-done.2) | copy-start | bytes 1179652
  682.3 9.1 %copy-start.5 = (bf16[768,256]{1,0:T(8,128)(2,1)S(1)}, bf16[768,256]{1,0:T(8,128)(2,1)}, u32[]{:S(2)}) copy-start(bf16[768,256]{1,0:T(8,128)(2,1)} %copy-done.4) | copy-start | bytes 1179652
  731.6 4.6 copy-start.6
Sparse Core Ops, SparseCore 0:
  561.5 88.2 reduce-scatter.1
